TPU v7x, 128 devices: a whole 4x4x4 slice. The times are simulated.
128 devices in a mesh: ex: 16 (over z, y), ey: 8 (over x, core).
Axes of the slice: x: 4, y: 4, z: 4, core: 2. Of those that a mesh axis runs over, the one named last changes fastest.
Arguments:
- tokens: bfloat16 [32768, 768], P(('ex', 'ey')), may hold values from -6 to 6
- routes: int32 [32768, 1], P(('ex', 'ey')), may hold values from 0 to 127; in each aligned block of 256 rows (0 to 255, 256 to 511, ...) at most 4 rows name the same one
- sub_expert: int32 [32768], P(('ex', 'ey')), may hold values from 0 to 1
- probability: float32 [32768], P(('ex', 'ey')), may hold values from 0.2 to 1
- weight_in: bfloat16 [256, 768, 3072], P(('ex', 'ey')), may hold values from -0.21875 to 0.21875
- weight_out: bfloat16 [256, 3072, 768], P(('ex', 'ey')), may hold values from -0.109375 to 0.109375
Outputs:
- mixed: bfloat16 [32768, 768], P(('ex', 'ey'))
Inputs may be any that keep to these rules, and one draw needn't show every extreme that they name: `routes`: among the 256 tokens of one device (aligned blocks of rows), no value is named by more than 4 tokens, a bound that some block reaches.
All inputs are finite; a program needn't handle non-finite values.
Results may differ from a plain program's by a relative error of at most 0.0058.
Values may be sent and summed in bfloat16 or wider, within the bound.
A program may use at most 64 MiB of HBM per device.

v0:
```python
import jax
import jax.numpy as jnp
from jax import lax
from jax.sharding import PartitionSpec as P


def local(tokens, routes, sub_expert, probability, weight_in, weight_out):
    count_ex = lax.axis_size("ex")
    count_ey = lax.axis_size("ey")
    devices_all = count_ex * count_ey
    local_experts = weight_in.shape[0]
    tok_rows = tokens.shape[0]
    width = tokens.shape[1]
    capacity = 2 * tok_rows // devices_all
    owner = routes[:, 0]
    label_key = owner * local_experts + sub_expert
    groups = local_experts * devices_all
    onehot = (label_key[:, None] == jnp.arange(groups, dtype=jnp.int32)[None, :]).astype(
        jnp.bfloat16
    )
    positions = jnp.arange(tok_rows, dtype=jnp.int32)
    earlier = (positions[:, None] > positions[None, :]).astype(jnp.bfloat16)
    before = jnp.dot(earlier, onehot, preferred_element_type=jnp.float32)
    slot = jnp.sum(before * onehot.astype(jnp.float32), axis=1).astype(jnp.int32)
    target = sub_expert * (devices_all * capacity) + owner * capacity + slot
    buffer_rows = jnp.arange(groups * capacity, dtype=jnp.int32)
    placing = (buffer_rows[:, None] == target[None, :]).astype(jnp.bfloat16)
    outgoing = jnp.dot(placing, tokens, preferred_element_type=jnp.float32).astype(jnp.bfloat16)
    arrive_rows = devices_all * capacity
    labels = jnp.full((groups * capacity,), local_experts, jnp.int32).at[target].set(sub_expert)
    shaped = outgoing.reshape(local_experts, devices_all, capacity, width)
    label_shaped = labels.reshape(local_experts, devices_all, capacity)
    arrived, labels_in = (
        lax.all_to_all(shaped, ("ex", "ey"), split_axis=1, concat_axis=1, tiled=True),
        lax.all_to_all(label_shaped, ("ex", "ey"), split_axis=1, concat_axis=1, tiled=True),
    )
    batch = arrived.reshape(local_experts, arrive_rows, width)
    hidden = jax.nn.relu(
        jnp.einsum("lrd,ldf->lrf", batch, weight_in, preferred_element_type=jnp.float32)
    ).astype(jnp.bfloat16)
    result = jnp.einsum(
        "lrf,lfd->lrd", hidden, weight_out, preferred_element_type=jnp.float32
    ).astype(jnp.bfloat16)
    shaped_back = result.reshape(local_experts, devices_all, capacity, width)
    returned = lax.all_to_all(shaped_back, ("ex", "ey"), split_axis=1, concat_axis=1, tiled=True)
    back_rows = returned.reshape(groups * capacity, width)
    gathered = jnp.einsum("rt,rd->td", placing, back_rows, preferred_element_type=jnp.float32)
    return (gathered * probability[:, None]).astype(jnp.bfloat16)


def solution(mesh):
    return jax.shard_map(
        local,
        mesh=mesh,
        in_specs=(
            P(("ex", "ey"), None),
            P(("ex", "ey"), None),
            P(("ex", "ey")),
            P(("ex", "ey")),
            P(("ex", "ey"), None, None),
            P(("ex", "ey"), None, None),
        ),
        out_specs=P(("ex", "ey"), None),
        check_vma=False,
    )
```

profile of v0, /device:TPU:1, one launch (start us, length us, event | category | flops | bytes accessed | tf_op | source)
XLA Modules:
  0.0 84.4 jit_solution(5231021807757352854)
XLA Ops:
  0.0 0.0 copy-start
  0.0 0.7 broadcast_multiply_fusion.1
  0.7 0.7 add.10
  1.4 0.3 fusion.2
  1.7 0.7 convert_add_fusion
  2.4 0.0 copy-done
  2.4 0.6 convolution_convert_fusion.1
  3.0 0.4 reshape.19
  3.4 0.0 copy-start.1
  3.4 0.5 copy.9
  3.9 36.2 %all_to_all.10 = bf16[2,128,4,768]{3,2,0,1:T(4,128)(2,1)S(1)} all-to-all(bf16[2,128,4,768]{3,2,0,1:T(4,128)(2,1)S(1)} %copy.9), channel_id=1, replica_groups=mesh['ex'=16,'ey'=8] {'ex','ey'}, dimensions={1} | all-to-all | bytes 3145728 | tf_op jit(solution)/shard_map/all_to_all | solution.py:34
  40.2 0.0 slice-start
  40.2 1.2 %copy.10 = bf16[2,128,4,768]{3,0,2,1:T(2,128)(2,1)S(1)} copy(bf16[2,128,4,768]{3,2,0,1:T(4,128)(2,1)S(1)} %all_to_all.10) | data formatting | bytes 3145728 | tf_op jit(solution)/shard_map/all_to_all | solution.py:34
  41.4 0.0 copy-done.1
  41.4 0.0 slice-start.1
  41.4 0.0 slice-start.2
  41.4 5.3 %maximum_convert_fusion = bf16[2,512,3072]{2,1,0:T(8,128)(2,1)S(1)} fusion(bf16[2,768,3072]{2,1,0:T(8,128)(2,1)S(1)} %copy-done.1, bf16[2,512,768]{2,0,1:T(2,128)(2,1)S(1)} %bitcast.8), kind=kOutput, calls=%fused_computation | convolution fusion | flops 4838129664 | bytes 17301504 | tf_op jit(solution)/shard_map/lrd,ldf->lrf/dot_general | solution.py:39
  46.8 0.0 slice-done
  46.8 0.0 slice-done.1
  46.8 0.0 slice-done.2
  46.8 5.1 %convolution_convert_fusion = bf16[2,512,768]{2,1,0:T(8,128)(2,1)S(1)} fusion(bf16[2,512,3072]{2,1,0:T(8,128)(2,1)S(1)} %maximum_convert_fusion, bf16[2,3072,768]{2,1,0:T(8,128)(2,1)S(1)} %bitcast.12), kind=kOutput, calls=%fused_computation.1 | convolution fusion | flops 4832624640 | bytes 17301504 | tf_op jit(solution)/shard_map/lrf,lfd->lrd/dot_general | solution.py:41
  51.9 0.4 reshape.21
  52.3 0.5 copy.12
  52.9 28.9 %all_to_all.11 = bf16[2,128,4,768]{3,2,0,1:T(4,128)(2,1)S(1)} all-to-all(bf16[2,128,4,768]{3,2,0,1:T(4,128)(2,1)S(1)} %copy.12), channel_id=1, replica_groups=mesh['ex'=16,'ey'=8] {'ex','ey'}, dimensions={1} | all-to-all | bytes 3145728 | tf_op jit(solution)/shard_map/all_to_all | solution.py:45
  81.8 0.5 copy.13
  82.3 0.0 copy-start.2
  82.3 0.4 reshape.22
  82.7 0.3 copy-done.2
  83.0 1.4 %fusion.1 = bf16[256,768]{1,0:T(8,128)(2,1)} fusion(bf16[1024,768]{1,0:T(8,128)(2,1)S(1)} %reshape.22, s32[256]{0:T(256)S(1)} %convert_add_fusion, f32[256]{0:T(256)S(1)} %copy-done.2), kind=kOutput, calls=%fused_computation.5 | convolution fusion | flops 403308544 | bytes 1968128 | tf_op jit(solution)/shard_map/rt,rd->td/dot_general | solution.py:47
  (1 shorter events, 0.0 us)
Async XLA Ops:
  0.0 2.4 %copy-start = (bf16[256,768]{1,0:T(8,128)(2,1)S(1)}, bf16[256,768]{1,0:T(8,128)(2,1)}, u32[]{:S(2)}) copy-start(bf16[256,768]{1,0:T(8,128)(2,1)} %param.6) | copy-start | bytes 1179652
  3.4 38.0 %copy-start.1 = (bf16[2,768,3072]{2,1,0:T(8,128)(2,1)S(1)}, bf16[2,768,3072]{2,1,0:T(8,128)(2,1)}, u32[]{:S(2)}) copy-start(bf16[2,768,3072]{2,1,0:T(8,128)(2,1)} %param.10) | copy-start | bytes 28311556
  40.2 6.6 %slice-start = ((s8[9437184]{0:T(1024)(128)(4,1)}), s8[4194304]{0:T(1024)(128)(4,1)S(1)}, s32[]{:S(2)}) async-start(s8[9437184]{0:T(1024)(128)(4,1)} %bitcast.11), calls=%async_computation.2 | async-start | bytes 8388608
  41.4 5.4 %slice-start.1 = ((s8[9437184]{0:T(1024)(128)(4,1)}), s8[4194304]{0:T(1024)(128)(4,1)S(1)}, s32[]{:S(2)}) async-start(s8[9437184]{0:T(1024)(128)(4,1)} %bitcast.11), calls=%async_computation.3 | async-start | bytes 8388608
  41.4 5.4 %slice-start.2 = ((s8[9437184]{0:T(1024)(128)(4,1)}), s8[1048576]{0:T(1024)(128)(4,1)S(1)}, s32[]{:S(2)}) async-start(s8[9437184]{0:T(1024)(128)(4,1)} %bitcast.11), calls=%async_computation.4 | async-start | bytes 2097152
  82.3 0.7 copy-start.2
where the time goes:
time: 84.6 us; the launch traced here: 84.4 us
  blocking collectives  65.1 us (77%)
  matrix products  12.7 us (15%)
  local copies, waits for them, and re-layouts  4.36 us (5%)
  other arithmetic  2.1 us (2%)
    all_to_all x1, blocking collectives, local(): lax.all_to_all(shaped, ('ex', 'ey'), split_axis=1, concat_axis=1, tiled=T...  36.2 us
    all_to_all x1, blocking collectives, local(): lax.all_to_all(shaped_back, ('ex', 'ey'), split_axis=1, concat_axis=1, ti...  28.9 us
    dot_general x1, matrix products, local(): jnp.einsum('lrd,ldf->lrf', batch, weight_in, preferred_element_type=jnp.f...  5.32 us
    dot_general x1, matrix products, local(): jnp.einsum('lrf,lfd->lrd', hidden, weight_out, preferred_element_type=jnp...  5.1 us

commit v1 on v0

--- a/solution.py
+++ b/solution.py
@@ -42,7 +42,15 @@
         "lrf,lfd->lrd", hidden, weight_out, preferred_element_type=jnp.float32
     ).astype(jnp.bfloat16)
     shaped_back = result.reshape(local_experts, devices_all, capacity, width)
-    returned = lax.all_to_all(shaped_back, ("ex", "ey"), split_axis=1, concat_axis=1, tiled=True)
+    returned = jnp.concatenate(
+        lax.all_to_all(
+            jnp.stack(jnp.split(shaped_back, lax.axis_size(("ex", "ey")), axis=1)),
+            ("ex", "ey"),
+            0,
+            0,
+        ),
+        axis=1,
+    )
     back_rows = returned.reshape(groups * capacity, width)
     gathered = jnp.einsum("rt,rd->td", placing, back_rows, preferred_element_type=jnp.float32)
     return (gathered * probability[:, None]).astype(jnp.bfloat16)

time: 84.6 us -> 92.4 us (1.092)
  matrix products: 12.7 us -> 19.1 us
    dot_general x1, matrix products: 5.32 us -> 9.08 us  [local(): jnp.einsum('lrd,ldf->lrf', batch, weight_in, preferred_element_type=jnp.f...]
    dot_general x1, matrix products: 5.1 us -> 7.77 us  [local(): jnp.einsum('lrf,lfd->lrd', hidden, weight_out, preferred_element_type=jnp...]
    unnamed x12 -> x131, local copies, waits for them, and re-layouts: 0.3 us -> 2 us
where the time goes in v1:
time: 92.4 us; the launch traced here: 92.2 us
  blocking collectives  65.1 us (70%)
  matrix products  19.1 us (21%)
  local copies, waits for them, and re-layouts  5.24 us (6%)
  other arithmetic  2.1 us (2%)
    all_to_all x1, blocking collectives, local(): lax.all_to_all(shaped, ('ex', 'ey'), split_axis=1, concat_axis=1, tiled=T...  36.2 us
    all_to_all x1, blocking collectives, local(): lax.all_to_all(jnp.stack(jnp.split(shaped_back, lax.axis_size(('ex', 'ey'...  28.9 us
    dot_general x1, matrix products, local(): jnp.einsum('lrd,ldf->lrf', batch, weight_in, preferred_element_type=jnp.f...  9.08 us
    dot_general x1, matrix products, local(): jnp.einsum('lrf,lfd->lrd', hidden, weight_out, preferred_element_type=jnp...  7.77 us
    unnamed x131, local copies, waits for them, and re-layouts  2 us

profile of v1, /device:TPU:1, one launch (start us, length us, event | category | flops | bytes accessed | tf_op | source)
XLA Modules:
  0.0 92.2 jit_solution(16543388121818346777)
XLA Ops:
  0.0 0.0 copy-start
  0.0 0.7 broadcast_multiply_fusion.1
  0.7 0.7 add.10
  1.4 0.3 fusion.1
  1.7 0.7 convert_add_fusion
  2.4 0.0 copy-done
  2.4 0.6 convolution_convert_fusion.1
  3.0 0.4 reshape.19
  3.4 0.5 copy.262
  3.9 36.2 %all_to_all.10 = bf16[2,128,4,768]{3,2,0,1:T(4,128)(2,1)S(1)} all-to-all(bf16[2,128,4,768]{3,2,0,1:T(4,128)(2,1)S(1)} %copy.262), channel_id=1, replica_groups=mesh['ex'=16,'ey'=8] {'ex','ey'}, dimensions={1} | all-to-all | bytes 3145728 | tf_op jit(solution)/shard_map/all_to_all | solution.py:34
  40.2 0.5 copy.263
  40.7 0.4 reshape.20
  41.1 9.1 %maximum_convert_fusion = bf16[2,512,3072]{2,1,0:T(8,128)(2,1)S(1)} fusion(bf16[2,512,768]{2,1,0:T(8,128)(2,1)S(1)} %reshape.20, bf16[2,768,3072]{2,1,0:T(8,128)(2,1)} %param.10), kind=kOutput, calls=%fused_computation | convolution fusion | flops 4838129664 | bytes 17301504 | tf_op jit(solution)/shard_map/lrd,ldf->lrf/dot_general | solution.py:39
  50.2 7.8 %convolution_convert_fusion = bf16[2,512,768]{2,1,0:T(8,128)(2,1)S(1)} fusion(bf16[2,512,3072]{2,1,0:T(8,128)(2,1)S(1)} %maximum_convert_fusion, bf16[2,3072,768]{2,1,0:T(8,128)(2,1)} %param.11), kind=kOutput, calls=%fused_computation.1 | convolution fusion | flops 4832624640 | bytes 17301504 | tf_op jit(solution)/shard_map/lrf,lfd->lrd/dot_general | solution.py:41
  58.0 0.4 reshape.21
  60.7 28.9 %all_to_all.11 = bf16[128,2,1,4,768]{4,3,1,2,0:T(4,128)(2,1)S(1)} all-to-all(bf16[128,2,1,4,768]{4,3,1,2,0:T(4,128)(2,1)S(1)} %constant_dynamic-update-slice_fusion), channel_id=1, replica_groups=mesh['ex'=16,'ey'=8] {'ex','ey'}, dimensions={0} | all-to-all | bytes 3145728 | tf_op jit(solution)/shard_map/all_to_all | solution.py:46
  89.5 0.5 copy.392
  90.1 0.0 copy-start.1
  90.1 0.4 reshape_reshape.3
  90.5 0.3 copy-done.1
  90.8 1.4 %fusion = bf16[256,768]{1,0:T(8,128)(2,1)} fusion(bf16[1024,768]{1,0:T(8,128)(2,1)S(1)} %reshape_reshape.3, s32[256]{0:T(256)S(1)} %convert_add_fusion, f32[256]{0:T(256)S(1)} %copy-done.1), kind=kOutput, calls=%fused_computation.4 | convolution fusion | flops 403308544 | bytes 1968128 | tf_op jit(solution)/shard_map/rt,rd->td/dot_general | solution.py:55
  (128 shorter events, 1.7 us)
Async XLA Ops:
  0.0 2.4 %copy-start = (bf16[256,768]{1,0:T(8,128)(2,1)S(1)}, bf16[256,768]{1,0:T(8,128)(2,1)}, u32[]{:S(2)}) copy-start(bf16[256,768]{1,0:T(8,128)(2,1)} %param.6) | copy-start | bytes 1179652
  90.1 0.7 copy-start.1
